TPU v7x, 32 devices: a whole 2x2x4 slice. The times are simulated.
32 devices in a mesh: tm: 8 (over z, core), space: 4 (over y, x).
Axes of the slice: x: 2, y: 2, z: 4, core: 2. Of those that a mesh axis runs over, the one named last changes fastest.
Arguments:
- solution: float32 [512, 384, 384], P('tm', 'space'), may hold values from -6 to 6
- residual: float32 [512, 384, 384], P('tm', 'space'), may hold values from -6 to 6
- direction: float32 [512, 384, 384], P('tm', 'space'), may hold values from -6 to 6
- reaction: float32 [512, 384, 384], P('tm', 'space'), may hold values from 0.1 to 2
- time_bands: float32 [2, 4, 512], replicated, may hold values from -0.25 to 1.1, as said below
- space_bands: float32 [2, 4, 384], replicated, may hold values from -0.25 to 1.1, as said below
- time_basis: float32 [512, 512], replicated, may hold values from -0.25 to 0.25
- space_basis: float32 [384, 384], replicated, may hold values from -0.3125 to 0.3125
- time_eigen: float32 [512], replicated, may hold values from 0.1 to 1
- space_eigen: float32 [384], replicated, may hold values from 0.1 to 1
Outputs:
- new_solution: float32 [512, 384, 384], P('tm', 'space')
- new_residual: float32 [512, 384, 384], P('tm', 'space')
- new_direction: float32 [512, 384, 384], P('tm', 'space')
Inputs may be any that keep to these rules, and one draw needn't show every extreme that they name: `time_bands`: each of the two matrices is symmetric with every diagonal entry larger than the sum of the magnitudes of the other entries of its row. `space_bands`: each of the two matrices is symmetric with every diagonal entry larger than the sum of the magnitudes of the other entries of its row.
All inputs are finite; a program needn't handle non-finite values.
Results may differ from a plain program's by a relative error of at most 0.000051.
Values sent between devices are 32-bit elements; how exact they have to be, the bound alone decides.
No kernel may reach another device: no remote copies, remote signals or barrier semaphores. Data moves between devices by JAX's collectives and lax.ppermute only.
A program may use at most 192 MiB of HBM per device.

v0:
```python
import jax
import jax.numpy as jnp
from jax import lax
from jax.sharding import PartitionSpec as P

highest = lax.Precision.HIGHEST


def extended_2(cells, sides, width):
    for axis, dim in sides:
        count = lax.axis_size(axis)
        ends = count - 1
        head = lax.slice_in_dim(cells, 0, width, axis=dim)
        tail = lax.slice_in_dim(cells, cells.shape[dim] - width, cells.shape[dim], axis=dim)
        cells = jnp.concatenate(
            [
                lax.ppermute(tail, axis, [(i, (i + 1) % count) for i in range(ends)]),
                cells,
                lax.ppermute(head, axis, [((i + 1) % count, i) for i in range(ends)]),
            ],
            axis=dim,
        )
    return cells


def band_apply(extended, band_rows, dimension):
    length = extended.shape[dimension] - 6
    target_shape = [1] * extended.ndim
    target_shape[dimension] = length

    def coefficient(which_row, first_row):
        return lax.slice_in_dim(band_rows[which_row], first_row, first_row + length).reshape(
            target_shape
        )

    def window(first_row):
        return lax.slice_in_dim(extended, first_row, first_row + length, axis=dimension)

    result = coefficient(0, 3) * window(3)
    for offset in (1, 2, 3):
        result = (
            result
            + coefficient(offset, 3) * window(3 + offset)
            + coefficient(offset, 3 - offset) * window(3 - offset)
        )
    return result


def pad_along(values, dimension):
    widths = [(0, 0)] * values.ndim
    widths[dimension] = (3, 3)
    return jnp.pad(values, widths)


def apply_operator(direction, reaction, time_bands, space_bands):
    rows_time = direction.shape[0]
    rows_space = direction.shape[1]
    halo_block = extended_2(direction, (("tm", 0), ("space", 1)), 3)
    padded_time = jnp.pad(time_bands, ((0, 0), (0, 0), (3, 3)))
    padded_space = jnp.pad(space_bands, ((0, 0), (0, 0), (3, 3)))
    time_rows = lax.dynamic_slice_in_dim(
        padded_time, lax.axis_index("tm") * rows_time, rows_time + 6, 2
    )
    space_rows = lax.dynamic_slice_in_dim(
        padded_space, lax.axis_index("space") * rows_space, rows_space + 6, 2
    )
    extended = pad_along(halo_block, 2)
    mass_y = band_apply(extended, padded_space[1], 2)
    stiff_y = band_apply(extended, padded_space[0], 2)
    mass_xy = band_apply(mass_y, space_rows[1], 1)
    stiff_x = band_apply(mass_y, space_rows[0], 1)
    stiff_yx = band_apply(stiff_y, space_rows[1], 1)
    temporal = band_apply(mass_xy, time_rows[0], 0) + band_apply(
        stiff_x + stiff_yx, time_rows[1], 0
    )
    return temporal + reaction * direction


def spectrum(time_eigen, space_eigen):
    time_count = lax.axis_size("tm")
    space_count = lax.axis_size("space")
    block_width = space_eigen.shape[0] // (time_count * space_count)
    group_index = lax.axis_index("space") * time_count + lax.axis_index("tm")
    block = lax.dynamic_slice_in_dim(space_eigen, group_index * block_width, block_width)
    return time_eigen[:, None, None] + space_eigen[None, :, None] + block[None, None, :]


def forward_fields(fields, time_basis, space_basis):
    along_y = jnp.einsum("ctxk,ka->ctxa", fields, space_basis, precision=highest)
    spread = lax.all_to_all(along_y, "space", split_axis=3, concat_axis=2, tiled=True)
    along_x = jnp.einsum("ctjy,jb->ctby", spread, space_basis, precision=highest)
    joined = lax.all_to_all(along_x, "tm", split_axis=3, concat_axis=1, tiled=True)
    return jnp.einsum("cixy,ia->caxy", joined, time_basis, precision=highest)


def inverse_fields(spectral, time_basis, space_basis):
    along_t = jnp.einsum("caxy,ia->cixy", spectral, time_basis, precision=highest)
    parted = lax.all_to_all(along_t, "tm", split_axis=1, concat_axis=3, tiled=True)
    along_x = jnp.einsum("ctby,jb->ctjy", parted, space_basis, precision=highest)
    blocks = lax.all_to_all(along_x, "space", split_axis=2, concat_axis=3, tiled=True)
    return jnp.einsum("ctxa,ka->ctxk", blocks, space_basis, precision=highest)


def per_device(
    solution,
    residual,
    direction,
    reaction,
    time_bands,
    space_bands,
    time_basis,
    space_basis,
    time_eigen,
    space_eigen,
):
    image = apply_operator(direction, reaction, time_bands, space_bands)
    eigen_sum = spectrum(time_eigen, space_eigen)
    both_hat = forward_fields(jnp.stack([residual, image]), time_basis, space_basis)
    first_scaled = both_hat[0] / eigen_sum
    image_scaled = both_hat[1] / eigen_sum
    norm_old, cross_term, image_norm, curvature = lax.psum(
        (
            jnp.sum(both_hat[0] * first_scaled),
            jnp.sum(both_hat[1] * first_scaled),
            jnp.sum(both_hat[1] * image_scaled),
            jnp.sum(direction * image),
        ),
        ("tm", "space"),
    )
    step_size = norm_old / curvature
    new_residual = residual - step_size * image
    spectral = first_scaled - step_size * image_scaled
    norm_new = norm_old - 2.0 * step_size * cross_term + step_size * step_size * image_norm
    precond = inverse_fields(spectral[None], time_basis, space_basis)[0]
    new_direction = precond + norm_new / norm_old * direction
    new_solution = solution + step_size * direction
    return (new_solution, new_residual, new_direction)


def solution(mesh):
    return jax.shard_map(
        per_device,
        mesh=mesh,
        in_specs=(
            P("tm", "space", None),
            P("tm", "space", None),
            P("tm", "space", None),
            P("tm", "space", None),
            P(),
            P(),
            P(),
            P(),
            P(),
            P(),
        ),
        out_specs=(P("tm", "space", None), P("tm", "space", None), P("tm", "space", None)),
        check_vma=False,
    )
```

profile of v0, /device:TPU:0, one launch (start us, length us, event | category | flops | bytes accessed | tf_op | source)
XLA Modules:
  0.0 1760.0 jit_solution(4880386826261498902)
XLA Ops:
  18.7 5.7 collective-permute-done.2
  24.4 11.1 collective-permute-done.3
  35.6 5.1 pad_maximum_fusion
  40.7 85.2 %multiply_add_fusion.1 = (f32[70,102,384]{2,1,0:T(8,128)}, f32[70,102,384]{2,1,0:T(8,128)}) fusion(f32[70,102,384]{2,1,0:T(8,128)} %pad_maximum_fusion, f32[384]{0:T(512)S(1)} %get-tuple-element.9, f32[384]{0:T(512)S(1)} %get-tuple-element.15, f32[384]{0:T(512)S(1)} %get-tuple-element.8, f32[384]{0:T(512)S(1)} %get-tuple-element.16, ...), kind=kLoop, calls=%fused_computation.18 | loop fusion | flops 71285760 | bytes 32922624 | tf_op jit(solution)/shard_map/add | solution.py:42
  125.9 31.0 %multiply_add_fusion.2 = f32[70,96,384]{2,1,0:T(8,128)} fusion(f32[70,102,384]{2,1,0:T(8,128)} %get-tuple-element.26, f32[96]{0:T(128)S(1)} %get-tuple-element.54, f32[96]{0:T(128)S(1)} %get-tuple-element.55, f32[96]{0:T(128)S(1)} %get-tuple-element.56, f32[96]{0:T(128)S(1)} %get-tuple-element.57, f32[96]{0:T(128)S(1)} %get-tuple-element.59, ...), kind=kLoop, calls=%fused_computation.33 | loop fusion | flops 33546240 | bytes 82578048 | tf_op jit(solution)/shard_map/add | solution.py:42
  156.9 56.5 %fusion.5 = f32[70,96,384]{2,1,0:T(8,128)} fusion(f32[70,102,384]{2,1,0:T(8,128)} %get-tuple-element.27, f32[70,102,384]{2,1,0:T(8,128)} %get-tuple-element.26, f32[96]{0:T(128)S(1)} %get-tuple-element.48, f32[96]{0:T(128)S(1)} %get-tuple-element.49, f32[96]{0:T(128)S(1)} %get-tuple-element.47, f32[96]{0:T(128)S(1)} %get-tuple-element.50, ...), kind=kLoop, calls=%fused_computation.21 | loop fusion | flops 69672960 | bytes 154834176 | tf_op jit(solution)/shard_map/add | solution.py:74
  213.5 55.2 %multiply_reduce_fusion = (f32[]{:T(128)}, f32[64,96,384]{2,1,0:T(8,128)}) fusion(f32[64,96,384]{2,1,0:T(8,128)} %param.12, f32[64,96,384]{2,1,0:T(8,128)} %param.13, f32[70,96,384]{2,1,0:T(8,128)} %fusion.5, f32[64]{0:T(128)S(1)} %get-tuple-element.38, f32[64]{0:T(128)S(1)} %get-tuple-element.39, f32[64]{0:T(128)S(1)} %get-tuple-element.37, ...), kind=kLoop, calls=%fused_computation.75 | loop fusion | flops 73138176 | bytes 160435712 | tf_op jit(solution)/shard_map/reduce_sum | solution.py:126
  268.7 40.4 %fusion = f32[2,64,96,384]{3,2,1,0:T(8,128)} fusion(f32[1,64,96,384]{3,2,1,0:T(8,128)} %bitcast.137, f32[1,64,96,384]{3,2,1,0:T(8,128)} %bitcast.141, f32[384,384]{1,0:T(8,128)S(1)} %copy-done.2), kind=kOutput, calls=%fused_computation.7 | convolution fusion | flops 21747990528 | bytes 38338560 | tf_op jit(solution)/shard_map/ctxk,ka->ctxa/dot_general | solution.py:89
  309.1 22.2 %copy.37 = f32[2,64,96,384]{2,1,0,3:T(8,128)} copy(f32[2,64,96,384]{3,2,1,0:T(8,128)} %fusion) | data formatting | bytes 37748736 | tf_op jit(solution)/shard_map/ctxk,ka->ctxa/dot_general | solution.py:89
  331.3 288.6 %all_to_all.66 = f32[2,64,96,384]{2,1,0,3:T(8,128)S(1)} all-to-all(f32[2,64,96,384]{2,1,0,3:T(8,128)} %copy.37), channel_id=1, replica_groups=mesh['tm'=8,'space'=4] {'space'}, dimensions={3} | all-to-all | bytes 37748736 | tf_op jit(solution)/shard_map/all_to_all | solution.py:90
  619.9 36.2 %copy.59 = f32[2,64,96,4,96]{2,3,4,1,0:T(4,128)} copy(f32[2,64,96,4,96]{2,1,0,4,3:T(8,128)S(1)} %bitcast.135) | data formatting | bytes 37748736 | tf_op jit(solution)/shard_map/all_to_all | solution.py:90
  656.2 26.3 %all_to_all.51 = f32[2,64,384,96]{2,3,1,0:T(8,128)} reshape(f32[2,64,4,96,96]{3,2,4,1,0:T(4,128)} %bitcast.136) | data formatting | bytes 37748736 | tf_op jit(solution)/shard_map/all_to_all | solution.py:90
  682.4 43.2 %convolution_bitcast_fusion.1 = f32[2,64,384,96]{2,3,1,0:T(8,128)S(1)} fusion(f32[2,64,384,96]{2,3,1,0:T(8,128)} %all_to_all.51, f32[384,384]{1,0:T(8,128)S(1)} %copy-done.2), kind=kOutput, calls=%fused_computation.80 | convolution fusion | flops 21743271936 | bytes 38338560 | tf_op jit(solution)/shard_map/ctjy,jb->ctby/dot_general | solution.py:91
  725.6 21.8 %copy.39 = f32[2,64,384,96]{2,1,0,3:T(8,128)} copy(f32[2,64,384,96]{2,3,1,0:T(8,128)S(1)} %convolution_bitcast_fusion.1) | data formatting | bytes 37748736 | tf_op jit(solution)/shard_map/ctjy,jb->ctby/transpose | solution.py:91
  747.5 9.2 all-to-all-start.1
  756.8 408.5 %all-to-all-done.1 = f32[2,64,384,96]{2,1,0,3:T(8,128)} async-done(((f32[2,64,384,96]{2,1,0,3:T(8,128)}), f32[2,64,384,96]{2,1,0,3:T(8,128)}, u32[]{:S(2)}, u32[]{:S(2)}) %all-to-all-start.1) | async-done | bytes 18874400 | tf_op jit(solution)/shard_map/all_to_all | solution.py:92
  1165.3 12.9 copy.41
  1178.2 35.3 %convolution_bitcast_fusion = f32[2,512,384,12]{1,2,3,0:T(8,128)S(1)} fusion(f32[2,512,384,12]{2,1,3,0:T(8,128)} %bitcast.134, f32[512,512]{1,0:T(8,128)S(1)} %copy-done), kind=kOutput, calls=%fused_computation.79 | convolution fusion | flops 28991029248 | bytes 38797312 | tf_op jit(solution)/shard_map/cixy,ia->caxy/dot_general | solution.py:93
  1213.5 6.5 copy-done.1
  1224.3 37.2 %all-reduce.3 = (f32[]{:T(128)}, f32[]{:T(128)}, f32[]{:T(128)}, f32[]{:T(128)}) all-reduce(f32[]{:T(128)} %get-tuple-element.5, f32[]{:T(128)} %get-tuple-element.24, f32[]{:T(128)} %get-tuple-element.4, f32[]{:T(128)} %get-tuple-element.3), channel_id=1, replica_groups=mesh['tm'=8,'space'=4] {'tm','space'}, use_global_device_ids=true, to_apply=%region_1.2 | all-reduce | flops 4 | bytes 32 | tf_op jit(solution)/shard_map/psum | solution.py:121
  1262.8 21.6 %fusion.44 = f32[1,512,384,12]{1,2,3,0:T(8,128)} fusion(f32[2,512,384,12]{1,2,3,0:T(8,128)} %copy-done.1, f32[]{:T(128)S(6)} %div.19, f32[12]{0:T(128)S(1)} %dynamic_slice.11, f32[512,384]{0,1:T(8,128)S(1)} %broadcast_add_fusion, f32[512,512]{1,0:T(8,128)S(1)} %copy-done), kind=kOutput, calls=%fused_computation.85 | convolution fusion | flops 14507311104 | bytes 30146612 | tf_op jit(solution)/shard_map/caxy,ia->cixy/dot_general | solution.py:97
  1284.4 23.1 %copy.43 = f32[1,512,384,12]{2,0,3,1:T(1,128)} copy(f32[1,512,384,12]{1,2,3,0:T(8,128)} %fusion.44) | data formatting | bytes 18874368 | tf_op jit(solution)/shard_map/caxy,ia->cixy/transpose | solution.py:97
  1307.5 210.6 %all_to_all.67 = f32[1,512,384,12]{2,0,3,1:T(1,128)S(1)} all-to-all(f32[1,512,384,12]{2,0,3,1:T(1,128)} %copy.43), channel_id=1, replica_groups=mesh['tm'=8,'space'=4] {'tm'}, dimensions={1} | all-to-all | bytes 18874368 | tf_op jit(solution)/shard_map/all_to_all | solution.py:98
  1527.0 24.3 %fusion.41 = f32[1,64,384,96]{2,3,1,0:T(8,128)} fusion(f32[64,384,96]{1,0,2:T(8,128)S(1)} %bitcast.138, f32[384,384]{1,0:T(8,128)S(1)} %copy-done.2), kind=kOutput, calls=%fused_computation.84 | convolution fusion | flops 10871635968 | bytes 19464192 | tf_op jit(solution)/shard_map/ctby,jb->ctjy/dot_general | solution.py:99
  1551.3 11.6 copy.47
  1562.9 6.6 all-to-all-start.3
  1572.0 12.0 multiply_subtract_fusion
  1584.0 12.0 multiply_add_fusion.4
  1596.0 111.5 %all-to-all-done.3 = f32[1,64,384,96]{3,1,0,2:T(8,128)} async-done(((f32[1,64,384,96]{3,1,0,2:T(8,128)}), f32[1,64,384,96]{3,1,0,2:T(8,128)}, u32[]{:S(2)}, u32[]{:S(2)}) %all-to-all-start.3) | async-done | bytes 9437216 | tf_op jit(solution)/shard_map/all_to_all | solution.py:100
  1707.4 16.4 copy.60
  1723.8 13.8 reshape.269
  1737.7 21.9 %multiply_add_fusion.3 = f32[64,96,384]{2,1,0:T(8,128)} fusion(f32[64,96,384]{2,1,0:T(8,128)} %param.12, f32[]{:T(128)S(6)} %div.23, f32[64,96,384]{2,1,0:T(8,128)} %reshape.269, f32[384,384]{1,0:T(8,128)S(1)} %copy-done.2), kind=kOutput, calls=%fused_computation.72 | convolution fusion | flops 10876354560 | bytes 28901380 | tf_op jit(solution)/shard_map/ctxa,ka->ctxk/dot_general | solution.py:101
  (34 shorter events, 31.4 us)
Async XLA Ops:
  0.6 1177.5 %copy-start = (f32[512,512]{1,0:T(8,128)S(1)}, f32[512,512]{1,0:T(8,128)}, u32[]{:S(2)}) copy-start(f32[512,512]{1,0:T(8,128)} %param.16) | copy-start | bytes 3145732
  1.9 5.7 collective-permute-start
  4.4 8.2 collective-permute-start.1
  7.6 10.7 copy-start.4
  7.7 10.9 copy-start.3
  12.8 11.6 collective-permute-start.2
  17.0 18.5 %collective-permute-start.3 = (f32[70,3,384]{2,1,0:T(4,128)S(1)}, f32[70,3,384]{2,1,0:T(4,128)S(1)}, u32[]{:S(2)}, u32[]{:S(2)}) collective-permute-start(f32[70,3,384]{2,1,0:T(4,128)S(1)} %get-tuple-element.29), channel_id=1, source_target_pairs={{1,0},{2,1},{3,2},{5,4},{6,5},{7,6},{9,8},{10,9},{11,10},{13,12},{... | collective-permute-start | bytes 967688 | tf_op jit(solution)/shard_map/ppermute | solution.py:19
  213.5 55.2 %copy-start.2 = (f32[384,384]{1,0:T(8,128)S(1)}, f32[384,384]{1,0:T(8,128)}, u32[]{:S(2)}) copy-start(f32[384,384]{1,0:T(8,128)} %param.17) | copy-start | bytes 1769476
  747.4 9.2 copy-start.5
  747.5 9.3 copy-start.6
  747.5 417.8 %all-to-all-start.1 = ((f32[2,64,384,96]{2,1,0,3:T(8,128)}), f32[2,64,384,96]{2,1,0,3:T(8,128)}, u32[]{:S(2)}, u32[]{:S(2)}) async-start(f32[2,64,384,96]{2,1,0,3:T(8,128)} %copy.39), calls=%async_computation.1 | async-start | bytes 37748736 | tf_op jit(solution)/shard_map/all_to_all | solution.py:92
  1213.5 6.5 copy-start.1
  1562.9 144.5 %all-to-all-start.3 = ((f32[1,64,384,96]{3,1,0,2:T(8,128)}), f32[1,64,384,96]{3,1,0,2:T(8,128)}, u32[]{:S(2)}, u32[]{:S(2)}) async-start(f32[1,64,384,96]{3,1,0,2:T(8,128)} %copy.47), calls=%async_computation.3 | async-start | bytes 25165824 | tf_op jit(solution)/shard_map/all_to_all | solution.py:100
where the time goes:
time: 1770 us; the launch traced here: 1760 us
  waiting for transfers between devices  537 us (30%)
  blocking collectives  536 us (30%)
  other arithmetic  262 us (15%)
  local copies, waits for them, and re-layouts  208 us (12%)
  matrix products  187 us (11%)
  starting transfers between devices  25 us (1%)
    all_to_all x1, waiting for transfers between devices, forward_fields(): lax.all_to_all(along_x, 'tm', split_axis=3, concat_axis=1, tiled=True)  408 us
    all_to_all x1, blocking collectives, forward_fields(): lax.all_to_all(along_y, 'space', split_axis=3, concat_axis=2, tiled=True)  289 us
    all_to_all x1, blocking collectives, inverse_fields(): lax.all_to_all(along_t, 'tm', split_axis=1, concat_axis=3, tiled=True)  211 us
    add x2, other arithmetic, band_apply(): result + coefficient(offset, 3) * window(3 + offset)  116 us
    all_to_all x1, waiting for transfers between devices, inverse_fields(): lax.all_to_all(along_x, 'space', split_axis=2, concat_axis=3, tiled=True)  111 us
    all_to_all x2, local copies, waits for them, and re-layouts, forward_fields(): lax.all_to_all(along_y, 'space', split_axis=3, concat_axis=2, tiled=True)  62.5 us
    add x1, other arithmetic, apply_operator(): stiff_x + stiff_yx  56.5 us
    reduce_sum x1, other arithmetic, per_device(): jnp.sum(direction * image)  55.2 us
  transfers between devices with their start and end apart: 6, of which 4 were waited for; matrix products, arithmetic and copies ran while one was open for 2% of the time, Pallas kernels for 0%

commit v1 on v0

--- a/solution.py
+++ b/solution.py
@@ -2,8 +2,18 @@
 import jax.numpy as jnp
 from jax import lax
 from jax.sharding import PartitionSpec as P
+from jax.lax import all_to_all, axis_size
 
 highest = lax.Precision.HIGHEST
+
+
+def apply_face_in(u_in, peer_axis, join_dim, k_dim):
+    return jnp.concatenate(
+        all_to_all(
+            jnp.stack(jnp.split(u_in, axis_size(peer_axis), axis=join_dim)), peer_axis, 0, 0
+        ),
+        axis=k_dim,
+    )
 
 
 def extended_2(cells, sides, width):
@@ -89,7 +99,7 @@
     along_y = jnp.einsum("ctxk,ka->ctxa", fields, space_basis, precision=highest)
     spread = lax.all_to_all(along_y, "space", split_axis=3, concat_axis=2, tiled=True)
     along_x = jnp.einsum("ctjy,jb->ctby", spread, space_basis, precision=highest)
-    joined = lax.all_to_all(along_x, "tm", split_axis=3, concat_axis=1, tiled=True)
+    joined = apply_face_in(along_x, "tm", 3, 1)
     return jnp.einsum("cixy,ia->caxy", joined, time_basis, precision=highest)
 
 

time: 1770 us -> 1790 us (1.011)
    transpose x1 -> x0, local copies, waits for them, and re-layouts: 21.8 us -> none  [forward_fields(): jnp.einsum('ctjy,jb->ctby', spread, space_basis, precision=highest)]
    another operation x1 -> x3, local copies, waits for them, and re-layouts: 13.8 us -> 34.3 us  [the longest x2 20.4 us: apply_face_in(): jnp.stack(jnp.split(u_in, axis_size(peer_axis), axis=join_dim))]
where the time goes in v1:
time: 1790 us; the launch traced here: 1770 us
  waiting for transfers between devices  537 us (30%)
  blocking collectives  536 us (30%)
  other arithmetic  262 us (15%)
  local copies, waits for them, and re-layouts  221 us (12%)
  matrix products  187 us (10%)
  starting transfers between devices  25 us (1%)
    all_to_all x1, waiting for transfers between devices, apply_face_in(): all_to_all(jnp.stack(jnp.split(u_in, axis_size(peer_axis), axis=join_dim)...  408 us
    all_to_all x1, blocking collectives, forward_fields(): lax.all_to_all(along_y, 'space', split_axis=3, concat_axis=2, tiled=True)  289 us
    all_to_all x1, blocking collectives, inverse_fields(): lax.all_to_all(along_t, 'tm', split_axis=1, concat_axis=3, tiled=True)  211 us
    add x2, other arithmetic, band_apply(): result + coefficient(offset, 3) * window(3 + offset)  116 us
    all_to_all x1, waiting for transfers between devices, inverse_fields(): lax.all_to_all(along_x, 'space', split_axis=2, concat_axis=3, tiled=True)  111 us
    all_to_all x2, local copies, waits for them, and re-layouts, forward_fields(): lax.all_to_all(along_y, 'space', split_axis=3, concat_axis=2, tiled=True)  62.5 us
    add x1, other arithmetic, apply_operator(): stiff_x + stiff_yx  56.5 us
    reduce_sum x1, other arithmetic, per_device(): jnp.sum(direction * image)  55.2 us
  transfers between devices with their start and end apart: 6, of which 4 were waited for; matrix products, arithmetic and copies ran while one was open for 2% of the time, Pallas kernels for 0%

profile of v1, /device:TPU:0, one launch (start us, length us, event | category | flops | bytes accessed | tf_op | source)
XLA Modules:
  0.0 1772.5 jit_solution(14855101598387709146)
XLA Ops:
  18.7 5.7 collective-permute-done.2
  24.4 11.1 collective-permute-done.3
  35.6 5.1 pad_maximum_fusion
  40.7 85.2 %multiply_add_fusion.1 = (f32[70,102,384]{2,1,0:T(8,128)}, f32[70,102,384]{2,1,0:T(8,128)}) fusion(f32[70,102,384]{2,1,0:T(8,128)} %pad_maximum_fusion, f32[384]{0:T(512)S(1)} %get-tuple-element.9, f32[384]{0:T(512)S(1)} %get-tuple-element.15, f32[384]{0:T(512)S(1)} %get-tuple-element.8, f32[384]{0:T(512)S(1)} %get-tuple-element.16, ...), kind=kLoop, calls=%fused_computation.18 | loop fusion | flops 71285760 | bytes 32922624 | tf_op jit(solution)/shard_map/add | solution.py:52
  125.9 31.0 %multiply_add_fusion.2 = f32[70,96,384]{2,1,0:T(8,128)} fusion(f32[70,102,384]{2,1,0:T(8,128)} %get-tuple-element.26, f32[96]{0:T(128)S(1)} %get-tuple-element.54, f32[96]{0:T(128)S(1)} %get-tuple-element.55, f32[96]{0:T(128)S(1)} %get-tuple-element.56, f32[96]{0:T(128)S(1)} %get-tuple-element.57, f32[96]{0:T(128)S(1)} %get-tuple-element.59, ...), kind=kLoop, calls=%fused_computation.33 | loop fusion | flops 33546240 | bytes 82578048 | tf_op jit(solution)/shard_map/add | solution.py:52
  156.9 56.5 %fusion.5 = f32[70,96,384]{2,1,0:T(8,128)} fusion(f32[70,102,384]{2,1,0:T(8,128)} %get-tuple-element.27, f32[70,102,384]{2,1,0:T(8,128)} %get-tuple-element.26, f32[96]{0:T(128)S(1)} %get-tuple-element.48, f32[96]{0:T(128)S(1)} %get-tuple-element.49, f32[96]{0:T(128)S(1)} %get-tuple-element.47, f32[96]{0:T(128)S(1)} %get-tuple-element.50, ...), kind=kLoop, calls=%fused_computation.21 | loop fusion | flops 69672960 | bytes 154834176 | tf_op jit(solution)/shard_map/add | solution.py:84
  213.5 55.2 %multiply_reduce_fusion = (f32[]{:T(128)}, f32[64,96,384]{2,1,0:T(8,128)}) fusion(f32[64,96,384]{2,1,0:T(8,128)} %param.12, f32[64,96,384]{2,1,0:T(8,128)} %param.13, f32[70,96,384]{2,1,0:T(8,128)} %fusion.5, f32[64]{0:T(128)S(1)} %get-tuple-element.38, f32[64]{0:T(128)S(1)} %get-tuple-element.39, f32[64]{0:T(128)S(1)} %get-tuple-element.37, ...), kind=kLoop, calls=%fused_computation.75 | loop fusion | flops 73138176 | bytes 160435712 | tf_op jit(solution)/shard_map/reduce_sum | solution.py:136
  268.7 40.4 %fusion = f32[2,64,96,384]{3,2,1,0:T(8,128)} fusion(f32[1,64,96,384]{3,2,1,0:T(8,128)} %bitcast.168, f32[1,64,96,384]{3,2,1,0:T(8,128)} %bitcast.172, f32[384,384]{1,0:T(8,128)S(1)} %copy-done.2), kind=kOutput, calls=%fused_computation.7 | convolution fusion | flops 21747990528 | bytes 38338560 | tf_op jit(solution)/shard_map/ctxk,ka->ctxa/dot_general | solution.py:99
  309.1 22.2 %copy.34 = f32[2,64,96,384]{2,1,0,3:T(8,128)} copy(f32[2,64,96,384]{3,2,1,0:T(8,128)} %fusion) | data formatting | bytes 37748736 | tf_op jit(solution)/shard_map/ctxk,ka->ctxa/dot_general | solution.py:99
  331.3 288.6 %all_to_all.53 = f32[2,64,96,384]{2,1,0,3:T(8,128)S(1)} all-to-all(f32[2,64,96,384]{2,1,0,3:T(8,128)} %copy.34), channel_id=1, replica_groups=mesh['tm'=8,'space'=4] {'space'}, dimensions={3} | all-to-all | bytes 37748736 | tf_op jit(solution)/shard_map/all_to_all | solution.py:100
  619.9 36.2 %copy.54 = f32[2,64,96,4,96]{2,3,4,1,0:T(4,128)} copy(f32[2,64,96,4,96]{2,1,0,4,3:T(8,128)S(1)} %bitcast.166) | data formatting | bytes 37748736 | tf_op jit(solution)/shard_map/all_to_all | solution.py:100
  656.2 26.3 %all_to_all.41 = f32[2,64,384,96]{2,3,1,0:T(8,128)} reshape(f32[2,64,4,96,96]{3,2,4,1,0:T(4,128)} %bitcast.167) | data formatting | bytes 37748736 | tf_op jit(solution)/shard_map/all_to_all | solution.py:100
  682.4 43.2 %convolution_bitcast_fusion.1 = f32[2,64,384,96]{2,3,1,0:T(8,128)S(1)} fusion(f32[2,64,384,96]{2,3,1,0:T(8,128)} %all_to_all.41, f32[384,384]{1,0:T(8,128)S(1)} %copy-done.2), kind=kOutput, calls=%fused_computation.80 | convolution fusion | flops 21743271936 | bytes 38338560 | tf_op jit(solution)/shard_map/ctjy,jb->ctby/dot_general | solution.py:101
  741.5 18.4 %copy.36 = f32[8,2,64,384,12]{3,2,4,1,0:T(8,128)} copy(f32[8,2,64,384,12]{3,4,2,1,0:T(8,128)} %fusion.47) | data formatting | bytes 37748736 | tf_op jit(solution)/shard_map/stack | solution.py:13
  760.0 9.2 all-to-all-start.1
  769.4 408.5 %all-to-all-done.1 = f32[8,2,64,384,12]{3,2,4,1,0:T(8,128)} async-done(((f32[8,2,64,384,12]{3,2,4,1,0:T(8,128)}), f32[8,2,64,384,12]{3,2,4,1,0:T(8,128)}, u32[]{:S(2)}, u32[]{:S(2)}) %all-to-all-start.1) | async-done | bytes 18874400 | tf_op jit(solution)/shard_map/all_to_all | solution.py:12
  1177.8 12.8 copy.37
  1190.7 35.3 %convolution_bitcast_fusion = f32[2,512,384,12]{1,2,3,0:T(8,128)S(1)} fusion(f32[2,512,384,12]{2,1,3,0:T(8,128)} %bitcast.165, f32[512,512]{1,0:T(8,128)S(1)} %copy-done), kind=kOutput, calls=%fused_computation.79 | convolution fusion | flops 28991029248 | bytes 38797312 | tf_op jit(solution)/shard_map/cixy,ia->caxy/dot_general | solution.py:103
  1226.0 6.5 copy-done.1
  1236.8 37.2 %all-reduce.3 = (f32[]{:T(128)}, f32[]{:T(128)}, f32[]{:T(128)}, f32[]{:T(128)}) all-reduce(f32[]{:T(128)} %get-tuple-element.5, f32[]{:T(128)} %get-tuple-element.24, f32[]{:T(128)} %get-tuple-element.4, f32[]{:T(128)} %get-tuple-element.3), channel_id=1, replica_groups=mesh['tm'=8,'space'=4] {'tm','space'}, use_global_device_ids=true, to_apply=%region_1.2 | all-reduce | flops 4 | bytes 32 | tf_op jit(solution)/shard_map/psum | solution.py:131
  1275.3 21.6 %fusion.44 = f32[1,512,384,12]{1,2,3,0:T(8,128)} fusion(f32[2,512,384,12]{1,2,3,0:T(8,128)} %copy-done.1, f32[]{:T(128)S(6)} %div.19, f32[12]{0:T(128)S(1)} %dynamic_slice.11, f32[512,384]{0,1:T(8,128)S(1)} %broadcast_add_fusion, f32[512,512]{1,0:T(8,128)S(1)} %copy-done), kind=kOutput, calls=%fused_computation.85 | convolution fusion | flops 14507311104 | bytes 30146612 | tf_op jit(solution)/shard_map/caxy,ia->cixy/dot_general | solution.py:107
  1296.9 23.1 %copy.39 = f32[1,512,384,12]{2,0,3,1:T(1,128)} copy(f32[1,512,384,12]{1,2,3,0:T(8,128)} %fusion.44) | data formatting | bytes 18874368 | tf_op jit(solution)/shard_map/caxy,ia->cixy/transpose | solution.py:107
  1320.0 210.6 %all_to_all.54 = f32[1,512,384,12]{2,0,3,1:T(1,128)S(1)} all-to-all(f32[1,512,384,12]{2,0,3,1:T(1,128)} %copy.39), channel_id=1, replica_groups=mesh['tm'=8,'space'=4] {'tm'}, dimensions={1} | all-to-all | bytes 18874368 | tf_op jit(solution)/shard_map/all_to_all | solution.py:108
  1539.5 24.3 %fusion.41 = f32[1,64,384,96]{2,3,1,0:T(8,128)} fusion(f32[64,384,96]{1,0,2:T(8,128)S(1)} %bitcast.169, f32[384,384]{1,0:T(8,128)S(1)} %copy-done.2), kind=kOutput, calls=%fused_computation.84 | convolution fusion | flops 10871635968 | bytes 19464192 | tf_op jit(solution)/shard_map/ctby,jb->ctjy/dot_general | solution.py:109
  1563.8 11.6 copy.43
  1575.4 6.6 all-to-all-start.3
  1584.5 12.0 multiply_subtract_fusion
  1596.5 12.0 multiply_add_fusion.4
  1608.5 111.5 %all-to-all-done.3 = f32[1,64,384,96]{3,1,0,2:T(8,128)} async-done(((f32[1,64,384,96]{3,1,0,2:T(8,128)}), f32[1,64,384,96]{3,1,0,2:T(8,128)}, u32[]{:S(2)}, u32[]{:S(2)}) %all-to-all-start.3) | async-done | bytes 9437216 | tf_op jit(solution)/shard_map/all_to_all | solution.py:110
  1719.9 16.4 copy.55
  1736.4 13.8 reshape.277
  1750.2 21.9 %multiply_add_fusion.3 = f32[64,96,384]{2,1,0:T(8,128)} fusion(f32[64,96,384]{2,1,0:T(8,128)} %param.12, f32[]{:T(128)S(6)} %div.23, f32[64,96,384]{2,1,0:T(8,128)} %reshape.277, f32[384,384]{1,0:T(8,128)S(1)} %copy-done.2), kind=kOutput, calls=%fused_computation.72 | convolution fusion | flops 10876354560 | bytes 28901380 | tf_op jit(solution)/shard_map/ctxa,ka->ctxk/dot_general | solution.py:111
  (42 shorter events, 47.4 us)
Async XLA Ops:
  0.6 1190.0 %copy-start = (f32[512,512]{1,0:T(8,128)S(1)}, f32[512,512]{1,0:T(8,128)}, u32[]{:S(2)}) copy-start(f32[512,512]{1,0:T(8,128)} %param.16) | copy-start | bytes 3145732
  1.9 5.7 collective-permute-start
  4.4 8.2 collective-permute-start.1
  7.6 10.7 copy-start.4
  7.7 10.9 copy-start.3
  12.8 11.6 collective-permute-start.2
  17.0 18.5 %collective-permute-start.3 = (f32[70,3,384]{2,1,0:T(4,128)S(1)}, f32[70,3,384]{2,1,0:T(4,128)S(1)}, u32[]{:S(2)}, u32[]{:S(2)}) collective-permute-start(f32[70,3,384]{2,1,0:T(4,128)S(1)} %get-tuple-element.29), channel_id=1, source_target_pairs={{1,0},{2,1},{3,2},{5,4},{6,5},{7,6},{9,8},{10,9},{11,10},{13,12},{... | collective-permute-start | bytes 967688 | tf_op jit(solution)/shard_map/ppermute | solution.py:29
  213.5 55.2 %copy-start.2 = (f32[384,384]{1,0:T(8,128)S(1)}, f32[384,384]{1,0:T(8,128)}, u32[]{:S(2)}) copy-start(f32[384,384]{1,0:T(8,128)} %param.17) | copy-start | bytes 1769476
  760.0 9.2 copy-start.5
  760.0 9.3 copy-start.6
  760.0 417.8 %all-to-all-start.1 = ((f32[8,2,64,384,12]{3,2,4,1,0:T(8,128)}), f32[8,2,64,384,12]{3,2,4,1,0:T(8,128)}, u32[]{:S(2)}, u32[]{:S(2)}) async-start(f32[8,2,64,384,12]{3,2,4,1,0:T(8,128)} %copy.36), calls=%async_computation.1 | async-start | bytes 37748736 | tf_op jit(solution)/shard_map/all_to_all | solution.py:12
  1226.0 6.5 copy-start.1
  1575.4 144.5 %all-to-all-start.3 = ((f32[1,64,384,96]{3,1,0,2:T(8,128)}), f32[1,64,384,96]{3,1,0,2:T(8,128)}, u32[]{:S(2)}, u32[]{:S(2)}) async-start(f32[1,64,384,96]{3,1,0,2:T(8,128)} %copy.43), calls=%async_computation.3 | async-start | bytes 25165824 | tf_op jit(solution)/shard_map/all_to_all | solution.py:110
